TPU v7x, 32 devices: a whole 2x2x4 slice. The times are simulated.
32 devices in a mesh: tx: 8 (over y, x, core), ty: 4 (over z).
Axes of the slice: x: 2, y: 2, z: 4, core: 2. Of those that a mesh axis runs over, the one named last changes fastest.
Arguments:
- velocity: bfloat16 [2, 60, 4, 8192], P(None, None, 'ty', 'tx'), may hold values from -6 to 6
- tracers: bfloat16 [2, 60, 4, 8192], P(None, None, 'ty', 'tx'), may hold values from -6 to 6
- surface_forcing: float32 [4, 4, 8192], P(None, 'ty', 'tx'), may hold values from -6 to 6
- thickness: float32 [60], replicated, may hold values from 0.5 to 2
- levels: int32 [4, 8192], P('ty', 'tx'), may hold values from 0 to 60, as said below
- surface_levels: int32 [128, 256], P('tx', 'ty'), may hold values from 0 to 60, as said below
- height: float32 [128, 256], P('tx', 'ty'), may hold values from -6 to 6
- transport: float32 [2, 128, 256], P(None, 'tx', 'ty'), may hold values from -12 to 12
- send_list: int32 [4, 8, 8, 128], P('ty', 'tx'), may hold values from -1 to 1023, as said below
- receive_cell: int32 [4, 8, 8, 128], P('ty', 'tx'), may hold values from -1 to 1023, as said below
- own_slot: int32 [128, 256], P('tx', 'ty'), may hold values from -1 to 1023, as said below
Outputs:
- new_velocity: bfloat16 [2, 60, 4, 8192], P(None, None, 'ty', 'tx')
- new_tracers: bfloat16 [2, 60, 4, 8192], P(None, None, 'ty', 'tx')
- new_height: float32 [128, 256], P('tx', 'ty')
- new_transport: float32 [2, 128, 256], P(None, 'tx', 'ty')
Inputs may be any that keep to these rules, and one draw needn't show every extreme that they name: levels and surface_levels describe one bathymetry: a slot's count equals that of its surface cell; 0 marks land. `surface_levels`: the same bathymetry as levels. send_list[j, i, d] lists distinct slots of tx index i, then -1; none for d = i; every pair i != d has at least one and at most 128 entries, exactly 128 for some pair in each tile column; as many columns go from i to d as from d to i; each slot is listed once or named by own_slot. receive_cell[j, d, i] holds as many entries as send_list[j, i, d], the cells of those columns in the same order, then -1; every cell of an area tile is named once here or has own_slot >= 0. `own_slot`: -1 where the column lies on another device.
All inputs are finite; a program needn't handle non-finite values.
Results may differ from a plain program's by a relative error of at most 0.001.
Values sent between devices are 32-bit elements; how exact they have to be, the bound alone decides.
A program may use at most 64 MiB of HBM per device.

v0:
```python
import functools

import jax
import jax.numpy as jnp
from jax import lax
from jax.experimental import pallas as pl
from jax.experimental.pallas import tpu as pltpu
from jax.sharding import PartitionSpec as P

LEV = 60
NSUB = 16
STEPS = 2

time_step = 0.5
coriolis = 0.3
mixing = 200.0
height_rate = 0.25
transport_rate = 0.9
depth_floor = 1.0

LANES = 128
HALO = NSUB * STEPS
OFFSETS = [(dx, dy) for dx in (-2, -1, 0, 1, 2) for dy in (-1, 0, 1) if (dx, dy) != (0, 0)]


def slot_of(dx, dy):
    return (dx + 2) * 3 + dy + 1


def split3(x):
    high = x.astype(jnp.bfloat16)
    rest = x - high.astype(jnp.float32)
    mid = rest.astype(jnp.bfloat16)
    low = (rest - mid.astype(jnp.float32)).astype(jnp.bfloat16)
    return high, mid, low


def one_hot(lane_idx):
    shape = (LANES, lane_idx.shape[1])
    hit = lax.broadcasted_iota(jnp.int32, shape, 0) == lane_idx
    return jnp.where(hit, 1.0, 0.0).astype(jnp.bfloat16)


def pack(values, count, row_idx, hot):
    rows = values.shape[0] // count
    entries = hot.shape[1]
    got = None
    for part in split3(values):
        term = jnp.dot(part, hot, preferred_element_type=jnp.float32)
        got = term if got is None else got + term
    got = got.reshape(count, rows, entries)
    hit = lax.broadcasted_iota(jnp.int32, (1, rows, entries), 1) == row_idx[None]
    return jnp.sum(jnp.where(hit, got, 0.0), axis=1)


def unpack(entries, rows, row_idx, hot):
    count, size = entries.shape
    hit = lax.broadcasted_iota(jnp.int32, (1, rows, size), 1) == row_idx[None]
    total = None
    for part in split3(entries):
        spread = jnp.where(hit, part.astype(jnp.float32)[:, None, :], 0.0)
        spread = spread.reshape(count * rows, size).astype(jnp.bfloat16)
        term = lax.dot_general(
            spread, hot, (((1,), (1,)), ((), ())), preferred_element_type=jnp.float32
        )
        total = term if total is None else total + term
    return total


def kernel(
    n_tx,
    n_ty,
    coef,
    vel,
    trc,
    forcing,
    levels,
    area_levels,
    area,
    slot_idx,
    cell_idx,
    out_vel,
    out_trc,
    out_area,
    low_s,
    inv_s,
    ratio_s,
    val,
    a2a_out,
    a2a_in,
    pair_out,
    right_out,
    left_out,
    pair_in,
    side_in,
    win,
    a2a_send,
    a2a_recv,
    halo_send,
    halo_recv,
):
    tx = lax.axis_index("tx")
    ty = lax.axis_index("ty")
    rows = area.shape[1]
    cols = LANES - 2 * HALO
    brows = forcing.shape[1]
    remote = n_tx * LANES
    local = rows * cols

    def present(dx, dy):
        return (tx + dx >= 0) & (tx + dx < n_tx) & (ty + dy >= 0) & (ty + dy < n_ty)

    barrier = pltpu.get_barrier_semaphore()

    def greet(step, carry):
        pl.semaphore_signal(
            barrier,
            inc=1,
            device_id={"tx": lax.rem(tx + step, n_tx), "ty": ty},
            device_id_type=pl.DeviceIdType.MESH,
        )
        return carry

    a2a_in[...] = jnp.zeros_like(a2a_in)
    pair_in[...] = jnp.zeros_like(pair_in)
    side_in[...] = jnp.zeros_like(side_in)

    lax.fori_loop(1, n_tx, greet, 0)
    for dx, dy in OFFSETS:
        if dy != 0:

            @pl.when(present(dx, dy))
            def _():
                pl.semaphore_signal(
                    barrier,
                    inc=1,
                    device_id={"tx": tx + dx, "ty": ty + dy},
                    device_id_type=pl.DeviceIdType.MESH,
                )

    lev = levels[...]
    wet0 = lev > 0

    def add_level(k, carry):
        su, sv, depth, area_depth = carry
        t = coef[0, k]
        wet = jnp.where(lev > k, t, 0.0)
        su = su + wet * vel[0, k].astype(jnp.float32)
        sv = sv + wet * vel[1, k].astype(jnp.float32)
        area_depth = area_depth + jnp.where(area_levels[...] > k, t, 0.0)
        return su, sv, depth + wet, area_depth

    zero = jnp.zeros((brows, LANES), jnp.float32)
    sum_u, sum_v, depth, area_depth = lax.fori_loop(
        0, LEV, add_level, (zero, zero, zero, jnp.zeros((rows, LANES), jnp.float32))
    )
    wind_x = jnp.where(wet0, forcing[0], 0.0)
    wind_y = jnp.where(wet0, forcing[1], 0.0)
    payload = jnp.concatenate([sum_u, sum_v, wind_x, wind_y], axis=0)

    def slots(start, size):
        idx = slot_idx[:, start : start + size]
        return idx >> 7, one_hot(idx & (LANES - 1))

    def cells(start, size):
        idx = cell_idx[:, start : start + size]
        return lax.div(idx + cols, cols) - 1, one_hot(lax.rem(idx + cols, cols))

    chunk = min(1024, remote)
    per_chunk = chunk // LANES
    chunks = range(0, remote, chunk)

    def exchange_copy(stage, peer, mine):
        return pltpu.make_async_remote_copy(
            src_ref=a2a_out.at[stage, peer],
            dst_ref=a2a_in.at[stage, mine],
            send_sem=a2a_send.at[stage, peer],
            recv_sem=a2a_recv.at[stage, mine],
            device_id={"tx": peer, "ty": ty},
            device_id_type=pl.DeviceIdType.MESH,
        )

    def start_exchange(stage):
        def go(step, carry):
            exchange_copy(stage, lax.rem(tx + step, n_tx), tx).start()
            return carry

        lax.fori_loop(1, n_tx, go, 0)

    def finish_exchange(stage):
        def go(step, carry):
            exchange_copy(stage, lax.rem(tx + step, n_tx), tx).wait_send()
            source = lax.rem(tx + step, n_tx)
            exchange_copy(stage, source, source).wait_recv()
            return carry

        lax.fori_loop(1, n_tx, go, 0)

    def stage_out(stage, first, packed):
        for block in range(per_chunk):
            a2a_out[stage, first // LANES + block] = packed[:, block * LANES : (block + 1) * LANES]

    def stage_in(stage, first):
        return jnp.concatenate(
            [a2a_in[stage, first // LANES + block] for block in range(per_chunk)], axis=1
        )

    for first in chunks:
        row_idx, hot = slots(first, chunk)
        stage_out(0, first, pack(payload, 4, row_idx, hot))

    greeted = jnp.int32(n_tx - 1)
    for dx, dy in OFFSETS:
        if dy != 0:
            greeted = greeted + jnp.where(present(dx, dy), 1, 0)
    pl.semaphore_wait(barrier, greeted)
    start_exchange(0)

    lane = lax.broadcasted_iota(jnp.int32, (rows, LANES), 1)

    def halo_copy(stage, dx, dy):
        there = slot_of(-dx, -dy)
        if dy == 0:
            src, dst = pair_out.at[stage], pair_in.at[stage, 2 - dx]
        else:
            src = (right_out if dy > 0 else left_out).at[stage]
            dst = side_in.at[stage, 2 - dx, 0 if dy > 0 else 1]
        return pltpu.make_async_remote_copy(
            src_ref=src,
            dst_ref=dst,
            send_sem=halo_send.at[stage, slot_of(dx, dy)],
            recv_sem=halo_recv.at[stage, there],
            device_id={"tx": tx + dx, "ty": ty + dy},
            device_id_type=pl.DeviceIdType.MESH,
        )

    def start_halo(stage, tiles):
        for half in range(2):
            pair_out[stage, half] = jnp.where(
                lane < cols, tiles[2 * half], pltpu.roll(tiles[2 * half + 1], cols, 1)
            )
        right = jnp.zeros((rows, LANES), jnp.float32)
        left = jnp.zeros((rows, LANES), jnp.float32)
        for f in range(4):
            here = (lane >= HALO * f) & (lane < HALO * (f + 1))
            shift = (HALO * f - (cols - HALO)) % LANES
            right = jnp.where(here, pltpu.roll(tiles[f], shift, 1) if shift else tiles[f], right)
            shift = HALO * f
            left = jnp.where(here, pltpu.roll(tiles[f], shift, 1) if shift else tiles[f], left)
        right_out[stage] = right
        left_out[stage] = left
        for dx, dy in OFFSETS:

            @pl.when(present(dx, dy))
            def _():
                halo_copy(stage, dx, dy).start()

    def roll_lanes(x, shift):
        shift = shift % LANES
        return pltpu.roll(x, shift, 1) if shift else x

    def finish_halo(stage, tiles):
        for dx, dy in OFFSETS:

            @pl.when(present(dx, dy))
            def _():
                halo_copy(stage, dx, dy).wait_send()
                halo_copy(stage, -dx, -dy).wait_recv()

        for dx in (-2, -1, 0, 1, 2):
            from_left = side_in[stage, dx + 2, 0]
            from_right = side_in[stage, dx + 2, 1]
            for f in range(4):
                if dx == 0:
                    middle = roll_lanes(tiles[f], HALO)
                else:
                    pair = pair_in[stage, dx + 2, f // 2]
                    middle = roll_lanes(pair, HALO if f % 2 == 0 else HALO - cols)
                block = jnp.where(
                    lane < HALO,
                    roll_lanes(from_left, -HALO * f),
                    jnp.where(
                        lane >= HALO + cols,
                        roll_lanes(from_right, HALO + cols - HALO * f),
                        middle,
                    ),
                )
                win[stage * 4 + f, (dx + 2) * rows : (dx + 3) * rows, :] = block

    state_tiles = [area[0], area[1], area[2], area_depth]
    start_halo(0, state_tiles)

    inv_top = coef[3, 0]
    heat = jnp.where(wet0, time_step * inv_top * forcing[2], 0.0)
    salt = jnp.where(wet0, time_step * inv_top * forcing[3], 0.0)
    push_x = time_step * inv_top * wind_x
    push_y = time_step * inv_top * wind_y
    tilt = time_step * coriolis

    def top_term(k, x):
        return jnp.where(k == 0, x, 0.0)

    def first_forward(k, carry):
        ratio, u, v, a, b = carry
        wet = lev > k
        low = jnp.where(wet, -coef[1, k], 0.0)
        upp = jnp.where(lev > k + 1, -coef[2, k], 0.0)
        inv = 1.0 / (1.0 - low - upp - low * ratio)
        ratio = upp * inv
        low_inv = low * inv
        ratio_s[k] = ratio
        low_s[k] = low_inv
        inv_s[k] = inv
        uu = vel[0, k].astype(jnp.float32)
        vv = vel[1, k].astype(jnp.float32)
        wet_inv = jnp.where(wet, inv, 0.0)
        u = (uu + tilt * vv + top_term(k, push_x)) * wet_inv - low_inv * u
        v = (vv - tilt * uu + top_term(k, push_y)) * wet_inv - low_inv * v
        a = (trc[0, k].astype(jnp.float32) + top_term(k, heat)) * wet_inv - low_inv * a
        b = (trc[1, k].astype(jnp.float32) + top_term(k, salt)) * wet_inv - low_inv * b
        val[0, k] = u
        val[1, k] = v
        val[2, k] = a
        val[3, k] = b
        return ratio, u, v, a, b

    lax.fori_loop(0, LEV, first_forward, (zero, zero, zero, zero, zero))

    def gather_area():
        total = None
        for first in chunks:
            row_idx, hot = cells(first, chunk)
            term = unpack(stage_in(0, first), rows, row_idx, hot)
            total = term if total is None else total + term
        return total

    own_row, own_hot = slots(remote, local)
    own_vals = pack(payload, 4, own_row, own_hot)
    cell_row, cell_hot = cells(remote, local)
    own_area = unpack(own_vals, rows, cell_row, cell_hot)
    finish_exchange(0)
    tile = own_area + gather_area()
    sum_tiles = [tile[f * rows : (f + 1) * rows] for f in range(4)]
    start_halo(1, sum_tiles)

    def first_backward(step, carry):
        k = LEV - 1 - step
        u, v, a, b, du, dv = carry
        ratio = ratio_s[k]
        t = coef[0, k]
        u = val[0, k] - ratio * u
        v = val[1, k] - ratio * v
        a = val[2, k] - ratio * a
        b = val[3, k] - ratio * b
        val[0, k] = u
        val[1, k] = v
        val[2, k] = a
        val[3, k] = b
        return u, v, a, b, du + t * u, dv + t * v

    mixed = lax.fori_loop(0, LEV, first_backward, (zero,) * 6)
    first_du, first_dv = mixed[4], mixed[5]

    def second_forward(k, carry):
        u, v, a, b = carry
        low_inv = low_s[k]
        wet_inv = jnp.where(lev > k, inv_s[k], 0.0)
        uu = val[0, k]
        vv = val[1, k]
        u = (uu + tilt * vv + top_term(k, push_x)) * wet_inv - low_inv * u
        v = (vv - tilt * uu + top_term(k, push_y)) * wet_inv - low_inv * v
        a = (val[2, k] + top_term(k, heat)) * wet_inv - low_inv * a
        b = (val[3, k] + top_term(k, salt)) * wet_inv - low_inv * b
        val[0, k] = u
        val[1, k] = v
        val[2, k] = a
        val[3, k] = b
        return u, v, a, b

    lax.fori_loop(0, LEV, second_forward, (zero,) * 4)

    def second_backward(step, carry):
        k = LEV - 1 - step
        u, v, a, b, du, dv = carry
        ratio = ratio_s[k]
        t = coef[0, k]
        u = val[0, k] - ratio * u
        v = val[1, k] - ratio * v
        a = val[2, k] - ratio * a
        b = val[3, k] - ratio * b
        val[0, k] = u
        val[1, k] = v
        out_trc[0, k] = a.astype(jnp.bfloat16)
        out_trc[1, k] = b.astype(jnp.bfloat16)
        return u, v, a, b, du + t * u, dv + t * v

    mixed = lax.fori_loop(0, LEV, second_backward, (zero,) * 6)
    second_du, second_dv = mixed[4], mixed[5]

    finish_halo(0, state_tiles)
    finish_halo(1, sum_tiles)
    wrows = 5 * rows
    depth_w = win[3]
    rate = transport_rate / LEV
    face_e = jnp.minimum(depth_w, pltpu.roll(depth_w, wrows - 1, 0))
    face_n = jnp.minimum(depth_w, pltpu.roll(depth_w, LANES - 1, 1))
    rate_e = rate * face_e
    rate_n = rate * face_n
    su, sv, wx, wy = win[4], win[5], win[6], win[7]
    state = (win[0], win[1], win[2])
    means = []
    filled = depth_w / jnp.maximum(depth_w, depth_floor)
    for ocean_step in range(STEPS):
        force_e = coriolis * sv + wx
        force_n = wy - coriolis * su
        push_e = rate * force_e
        push_n = rate * force_n

        def substep(counter, carry):
            h, e, n, te, tn = carry
            spread = e - pltpu.roll(e, 1, 0) + n - pltpu.roll(n, 1, 1)
            h = h - height_rate * spread
            slope_e = pltpu.roll(h, wrows - 1, 0) - h
            slope_n = pltpu.roll(h, LANES - 1, 1) - h
            e = jnp.where(rate_e > 0, e + (push_e - rate_e * slope_e), 0.0)
            n = jnp.where(rate_n > 0, n + (push_n - rate_n * slope_n), 0.0)
            return h, e, n, te + e, tn + n

        nothing = jnp.zeros((wrows, LANES), jnp.float32)
        h, e, n, te, tn = lax.fori_loop(0, NSUB, substep, state + (nothing, nothing))
        state = (h, e, n)
        mean_e = te / NSUB
        mean_n = tn / NSUB
        means += [mean_e, mean_n]
        if ocean_step + 1 < STEPS:
            du = su + time_step * force_e
            dv = sv + time_step * force_n
            su = du + (mean_e - du) * filled
            sv = dv + (mean_n - dv) * filled

    def centre(x):
        return roll_lanes(x[2 * rows : 3 * rows], -HALO)

    flow = jnp.concatenate([centre(x) for x in means], axis=0)
    for first in chunks:
        row_idx, hot = cells(first, chunk)
        stage_out(1, first, pack(flow, 4, row_idx, hot))
    start_exchange(1)
    for f in range(3):
        out_area[f] = centre(state[f])
    slot_flow = unpack(pack(flow, 4, cell_row, cell_hot), brows, own_row, own_hot)
    finish_exchange(1)
    for first in chunks:
        row_idx, hot = slots(first, chunk)
        slot_flow = slot_flow + unpack(stage_in(1, first), brows, row_idx, hot)

    floor = jnp.maximum(depth, depth_floor)
    shift_u = (slot_flow[0:brows] - first_du) / floor
    shift_v = (slot_flow[brows : 2 * brows] - first_dv) / floor
    carry_u = shift_u + tilt * shift_v
    carry_v = shift_v - tilt * shift_u
    last_u = carry_u + (slot_flow[2 * brows : 3 * brows] - second_du - depth * carry_u) / floor
    last_v = carry_v + (slot_flow[3 * brows :] - second_dv - depth * carry_v) / floor

    def finish(k, carry):
        wet = lev > k
        out_vel[0, k] = (val[0, k] + jnp.where(wet, last_u, 0.0)).astype(jnp.bfloat16)
        out_vel[1, k] = (val[1, k] + jnp.where(wet, last_v, 0.0)).astype(jnp.bfloat16)
        return carry

    lax.fori_loop(0, LEV, finish, 0)


def body(
    n_tx,
    n_ty,
    velocity,
    tracers,
    surface_forcing,
    thickness,
    levels,
    surface_levels,
    height,
    transport,
    send_list,
    receive_cell,
    own_slot,
):
    rows, cols = height.shape
    slots = levels.shape[1]
    brows = slots // LANES
    cap = send_list.shape[3]
    vel = velocity.reshape(2, LEV, brows, LANES)
    trc = tracers.reshape(2, LEV, brows, LANES)
    forcing = surface_forcing.reshape(4, brows, LANES)
    gap = (0.5 * 2.0 * mixing) / (thickness[:-1] + thickness[1:])
    none = jnp.zeros((1,), jnp.float32)
    coef = jnp.stack(
        [
            thickness,
            jnp.concatenate([none, gap]) / thickness,
            jnp.concatenate([gap, none]) / thickness,
            1.0 / thickness,
        ]
    )
    pad = ((0, 0), (0, 0), (0, LANES - cap))
    sends = jnp.pad(send_list[0], pad, constant_values=-1).reshape(1, -1)
    receives = jnp.pad(receive_cell[0], pad, constant_values=-1).reshape(1, -1)
    slot_idx = jnp.concatenate([sends, own_slot.reshape(1, -1)], axis=1)
    cell_idx = jnp.concatenate(
        [receives, lax.broadcasted_iota(jnp.int32, (1, rows * cols), 1)], axis=1
    )
    area = jnp.concatenate([height[None], transport], axis=0)
    area = jnp.pad(area, ((0, 0), (0, 0), (0, LANES - cols)))
    area_levels = jnp.pad(surface_levels, ((0, 0), (0, LANES - cols)))
    vmem = pl.BlockSpec(memory_space=pltpu.VMEM)
    smem = pl.BlockSpec(memory_space=pltpu.SMEM)
    f32 = jnp.float32
    column = pltpu.VMEM((LEV, brows, LANES), f32)
    new_vel, new_trc, new_area = pl.pallas_call(
        functools.partial(kernel, n_tx, n_ty),
        out_shape=(
            jax.ShapeDtypeStruct((2, LEV, brows, LANES), jnp.bfloat16),
            jax.ShapeDtypeStruct((2, LEV, brows, LANES), jnp.bfloat16),
            jax.ShapeDtypeStruct((3, rows, LANES), f32),
        ),
        in_specs=[smem] + [vmem] * 8,
        out_specs=(vmem, vmem, vmem),
        scratch_shapes=[
            column,
            column,
            column,
            pltpu.VMEM((4, LEV, brows, LANES), f32),
            pltpu.VMEM((2, n_tx, 4, LANES), f32),
            pltpu.VMEM((2, n_tx, 4, LANES), f32),
            pltpu.VMEM((2, 2, rows, LANES), f32),
            pltpu.VMEM((2, rows, LANES), f32),
            pltpu.VMEM((2, rows, LANES), f32),
            pltpu.VMEM((2, 5, 2, rows, LANES), f32),
            pltpu.VMEM((2, 5, 2, rows, LANES), f32),
            pltpu.VMEM((8, 5 * rows, LANES), f32),
            pltpu.SemaphoreType.DMA((2, n_tx)),
            pltpu.SemaphoreType.DMA((2, n_tx)),
            pltpu.SemaphoreType.DMA((2, 15)),
            pltpu.SemaphoreType.DMA((2, 15)),
        ],
        compiler_params=pltpu.CompilerParams(
            collective_id=0, has_side_effects=True, vmem_limit_bytes=48 * 1024 * 1024
        ),
        name="ocean",
    )(coef, vel, trc, forcing, levels.reshape(brows, LANES), area_levels, area, slot_idx, cell_idx)
    new_velocity = new_vel.reshape(2, LEV, 1, slots)
    new_tracers = new_trc.reshape(2, LEV, 1, slots)
    return (new_velocity, new_tracers, new_area[0, :, :cols], new_area[1:, :, :cols])


def solution(mesh):
    in_specs = (
        P(None, None, "ty", "tx"),
        P(None, None, "ty", "tx"),
        P(None, "ty", "tx"),
        P(),
        P("ty", "tx"),
        P("tx", "ty"),
        P("tx", "ty"),
        P(None, "tx", "ty"),
        P("ty", "tx", None, None),
        P("ty", "tx", None, None),
        P("tx", "ty"),
    )
    out_specs = (
        P(None, None, "ty", "tx"),
        P(None, None, "ty", "tx"),
        P("tx", "ty"),
        P(None, "tx", "ty"),
    )
    return jax.shard_map(
        functools.partial(body, mesh.shape["tx"], mesh.shape["ty"]),
        mesh=mesh,
        in_specs=in_specs,
        out_specs=out_specs,
        check_vma=False,
    )
```

profile of v0, /device:TPU:0, one launch (start us, length us, event | category | flops | bytes accessed | tf_op | source)
XLA Modules:
  0.0 33.7 jit_solution(2044520740125247174)
XLA Ops:
  0.6 0.0 copy-start.9
  0.6 0.0 copy-start.4
  0.7 0.6 %copy-done.9 = f32[60]{0:T(128)S(1)} copy-done((f32[60]{0:T(128)S(1)}, f32[60]{0:T(128)}, u32[]{:S(2)}) %copy-start.9) | copy-done | bytes 264
  1.3 0.1 add_divide_fusion
  1.4 0.1 fusion.1
  1.5 0.0 copy-done.4
  1.5 0.0 copy-start.5
  1.5 0.1 reshape.42
  1.6 0.6 %copy-done.5 = s32[16,64]{1,0:T(8,128)S(1)} copy-done((s32[16,64]{1,0:T(8,128)S(1)}, s32[16,64]{1,0:T(8,128)}, u32[]{:S(2)}) %copy-start.5) | copy-done | bytes 4120
  2.2 0.0 copy-start.7
  2.2 0.0 copy-start.8
  2.2 0.7 %copy-done.7 = s32[1,1,8,128]{3,2,1,0:T(8,128)S(1)} copy-done((s32[1,1,8,128]{3,2,1,0:T(8,128)S(1)}, s32[1,1,8,128]{3,2,1,0:T(8,128)}, u32[]{:S(2)}) %copy-start.7) | copy-done | bytes 4120
  2.9 0.0 copy-done.8
  2.9 0.0 copy-start.3
  2.9 0.0 copy-start.6
  2.9 0.7 %copy-done.3 = f32[2,16,64]{2,1,0:T(8,128)S(1)} copy-done((f32[2,16,64]{2,1,0:T(8,128)S(1)}, f32[2,16,64]{2,1,0:T(8,128)}, u32[]{:S(2)}) %copy-start.3) | copy-done | bytes 8216
  3.6 0.0 copy-done.6
  3.6 1.1 %reshape.37 = bf16[2,60,8,128]{3,2,0,1:T(8,128)(2,1)S(1)} reshape(bf16[2,60,1,1024]{3,0,2,1:T(2,128)(2,1)} %param.11) | data formatting | bytes 491520 | tf_op jit(solution)/shard_map/reshape | solution.py:493
  4.7 0.0 copy-start.2
  4.7 0.9 %copy-done.2 = bf16[2,60,1,1024]{3,0,2,1:T(2,128)(2,1)S(1)} copy-done((bf16[2,60,1,1024]{3,0,2,1:T(2,128)(2,1)S(1)}, bf16[2,60,1,1024]{3,0,2,1:T(2,128)(2,1)}, u32[]{:S(2)}) %copy-start.2) | copy-done | bytes 245784
  5.7 0.2 reshape.38
  5.8 0.0 copy-start
  5.8 0.0 copy-start.1
  5.9 0.7 %copy-done = f32[4,1,1024]{2,1,0:T(1,128)S(1)} copy-done((f32[4,1,1024]{2,1,0:T(1,128)S(1)}, f32[4,1,1024]{2,1,0:T(1,128)}, u32[]{:S(2)}) %copy-start) | copy-done | bytes 16408
  6.5 0.0 copy-done.1
  6.5 23.8 %ocean.1 = (bf16[2,60,8,128]{3,2,1,0:T(8,128)(2,1)S(1)}, bf16[2,60,8,128]{3,2,1,0:T(8,128)(2,1)S(1)}, f32[3,16,128]{2,1,0:T(8,128)S(1)}) custom-call(f32[4,60]{1,0:T(4,128)S(1)} %pad_maximum_fusion.coef, bf16[2,60,8,128]{3,2,1,0:T(8,128)(2,1)S(1)} %copy.19.vel, bf16[2,60,8,128]{3,2,1,0:T(8,128)(2,1)S(1)} %copy.20.trc, f32[4,8,128]{2,1,0:T(8,128)S(1)} %bitcast.22, ...), custom_call_target="tpu_custom_call" | custom-call | tf_op jit(solution)/shard_map/ocean/pallas_call | solution.py:520
  30.4 0.6 %slice_bitcast_fusion = f32[16,64]{1,0:T(8,128)} fusion(f32[3,16,128]{2,1,0:T(8,128)S(1)} %get-tuple-element.9), kind=kLoop, calls=%fused_computation.4 | loop fusion | bytes 8192 | tf_op jit(solution)/shard_map/squeeze | solution.py:554
  31.0 0.6 %slice.15 = f32[2,16,64]{2,1,0:T(8,128)} slice(f32[3,16,128]{2,1,0:T(8,128)S(1)} %get-tuple-element.9), slice={[1:3], [0:16], [0:64]} | slice | bytes 16384 | tf_op jit(solution)/shard_map/slice | solution.py:554
  31.6 0.1 reshape.46
  31.7 0.9 %copy.23 = bf16[2,60,1,1024]{3,0,2,1:T(2,128)(2,1)} copy(bf16[2,60,1,1024]{3,1,0,2:T(8,128)(2,1)S(1)} %reshape.46) | data formatting | bytes 491520
  32.6 0.1 reshape.47
  32.8 0.9 %copy.24 = bf16[2,60,1,1024]{3,0,2,1:T(2,128)(2,1)} copy(bf16[2,60,1,1024]{3,1,0,2:T(8,128)(2,1)S(1)} %reshape.47) | data formatting | bytes 491520
  (7 shorter events, 0.1 us)
Async XLA Ops:
  0.6 0.7 %copy-start.9 = (f32[60]{0:T(128)S(1)}, f32[60]{0:T(128)}, u32[]{:S(2)}) copy-start(f32[60]{0:T(128)} %param.14) | copy-start | bytes 724
  0.6 0.8 %copy-start.4 = (s32[16,64]{1,0:T(8,128)S(1)}, s32[16,64]{1,0:T(8,128)}, u32[]{:S(2)}) copy-start(s32[16,64]{1,0:T(8,128)} %param.21) | copy-start | bytes 12292
  1.5 0.7 %copy-start.5 = (s32[16,64]{1,0:T(8,128)S(1)}, s32[16,64]{1,0:T(8,128)}, u32[]{:S(2)}) copy-start(s32[16,64]{1,0:T(8,128)} %param.16) | copy-start | bytes 12292
  2.2 0.7 %copy-start.7 = (s32[1,1,8,128]{3,2,1,0:T(8,128)S(1)}, s32[1,1,8,128]{3,2,1,0:T(8,128)}, u32[]{:S(2)}) copy-start(s32[1,1,8,128]{3,2,1,0:T(8,128)} %param.19) | copy-start | bytes 12292
  2.2 0.7 %copy-start.8 = (s32[1,1,8,128]{3,2,1,0:T(8,128)S(1)}, s32[1,1,8,128]{3,2,1,0:T(8,128)}, u32[]{:S(2)}) copy-start(s32[1,1,8,128]{3,2,1,0:T(8,128)} %param.20) | copy-start | bytes 12292
  2.9 0.7 %copy-start.3 = (f32[2,16,64]{2,1,0:T(8,128)S(1)}, f32[2,16,64]{2,1,0:T(8,128)}, u32[]{:S(2)}) copy-start(f32[2,16,64]{2,1,0:T(8,128)} %param.18) | copy-start | bytes 24580
  2.9 0.7 %copy-start.6 = (f32[16,64]{1,0:T(8,128)S(1)}, f32[16,64]{1,0:T(8,128)}, u32[]{:S(2)}) copy-start(f32[16,64]{1,0:T(8,128)} %param.17) | copy-start | bytes 12292
  4.7 0.9 %copy-start.2 = (bf16[2,60,1,1024]{3,0,2,1:T(2,128)(2,1)S(1)}, bf16[2,60,1,1024]{3,0,2,1:T(2,128)(2,1)}, u32[]{:S(2)}) copy-start(bf16[2,60,1,1024]{3,0,2,1:T(2,128)(2,1)} %param.12) | copy-start | bytes 737284
  5.8 0.7 %copy-start = (f32[4,1,1024]{2,1,0:T(1,128)S(1)}, f32[4,1,1024]{2,1,0:T(1,128)}, u32[]{:S(2)}) copy-start(f32[4,1,1024]{2,1,0:T(1,128)} %param.13) | copy-start | bytes 49156
  5.8 0.7 %copy-start.1 = (s32[1,1024]{1,0:T(1,128)S(1)}, s32[1,1024]{1,0:T(1,128)}, u32[]{:S(2)}) copy-start(s32[1,1024]{1,0:T(1,128)} %param.15) | copy-start | bytes 12292
where the time goes:
time: 34.2 us; the launch traced here: 33.7 us
  Pallas kernels  23.8 us (70%)
  local copies, waits for them, and re-layouts  9.01 us (26%)
  between operations  0.74 us (2%)
    pallas_call x1, Pallas kernels, body(): pl.pallas_call(functools.partial(kernel, n_tx, n_ty), out_shape=(jax.Shap...  23.8 us
    unnamed x22, local copies, waits for them, and re-layouts  6.15 us
    reshape x2, local copies, waits for them, and re-layouts, body(): vel = velocity.reshape(2, LEV, brows, LANES)  1.12 us

commit v1 on v0

--- a/solution.py
+++ b/solution.py
@@ -70,18 +70,36 @@
 def kernel(
     n_tx,
     n_ty,
+    thick_hbm,
+    vel_hbm,
+    trc_hbm,
+    forcing_hbm,
+    levels_hbm,
+    area_levels_hbm,
+    height_hbm,
+    transport_hbm,
+    send_hbm,
+    receive_hbm,
+    own_hbm,
+    out_vel,
+    out_trc,
+    out_height,
+    out_transport,
+    thick_in,
+    vel_in,
+    trc_in,
+    forcing,
+    levels,
+    area_levels_in,
+    height_in,
+    transport_in,
+    send_in,
+    receive_in,
+    own_in,
+    in_sem,
     coef,
     vel,
     trc,
-    forcing,
-    levels,
-    area_levels,
-    area,
-    slot_idx,
-    cell_idx,
-    out_vel,
-    out_trc,
-    out_area,
     low_s,
     inv_s,
     ratio_s,
@@ -101,7 +119,7 @@
 ):
     tx = lax.axis_index("tx")
     ty = lax.axis_index("ty")
-    rows = area.shape[1]
+    rows = height_in.shape[0]
     cols = LANES - 2 * HALO
     brows = forcing.shape[1]
     remote = n_tx * LANES
@@ -109,6 +127,23 @@
 
     def present(dx, dy):
         return (tx + dx >= 0) & (tx + dx < n_tx) & (ty + dy >= 0) & (ty + dy < n_ty)
+
+    def fetch(number, src, dst):
+        copy = pltpu.make_async_copy(src, dst, in_sem.at[number])
+        copy.start()
+        return copy
+
+    vel_copy = fetch(0, vel_hbm, vel_in)
+    thick_copy = fetch(1, thick_hbm, thick_in)
+    level_copy = fetch(2, levels_hbm, levels)
+    area_level_copy = fetch(3, area_levels_hbm, area_levels_in)
+    forcing_copy = fetch(4, forcing_hbm, forcing)
+    send_copy = fetch(5, send_hbm, send_in)
+    height_copy = fetch(6, height_hbm, height_in)
+    transport_copy = fetch(7, transport_hbm, transport_in)
+    trc_copy = fetch(8, trc_hbm, trc_in)
+    receive_copy = fetch(9, receive_hbm, receive_in)
+    own_copy = fetch(10, own_hbm, own_in)
 
     barrier = pltpu.get_barrier_semaphore()
 
@@ -138,33 +173,98 @@
                     device_id_type=pl.DeviceIdType.MESH,
                 )
 
+    thick_copy.wait()
+    size = coef.shape[1]
+    row_at = lax.broadcasted_iota(jnp.int32, (size, LANES), 0)
+    lane_at = lax.broadcasted_iota(jnp.int32, (size, LANES), 1)
+    row = thick_in[...]
+    row = jnp.concatenate([row, jnp.ones((1, LANES - LEV), jnp.float32)], axis=1)
+
+    def along_rows(x):
+        column = jnp.sum(jnp.where(row_at == lane_at, x, 0.0), axis=1, keepdims=True)
+        return jnp.broadcast_to(column, (size, LANES))
+
+    thick = along_rows(row)
+    gap = jnp.where(
+        lane_at[:1] < LEV - 1, mixing / (row + pltpu.roll(row, LANES - 1, 1)), 0.0
+    )
+    coef[0] = thick
+    coef[1] = along_rows(pltpu.roll(gap, 1, 1)) / thick
+    coef[2] = along_rows(gap) / thick
+
+    def at_level(which, k):
+        return jnp.broadcast_to(coef[which, pl.ds(k, 1), :], (brows, LANES))
+
+    def pair(ref, k):
+        first = pl.multiple_of(k * 2 * brows, 2 * brows)
+        return (
+            ref[pl.ds(first, brows, stride=2), :],
+            ref[pl.ds(first + 1, brows, stride=2), :],
+        )
+
+    def put_pair(ref, k, one, two):
+        first = pl.multiple_of(k * 2 * brows, 2 * brows)
+        ref[pl.ds(first, brows, stride=2), :] = one
+        ref[pl.ds(first + 1, brows, stride=2), :] = two
+
+    def sweep(step, carry, unroll):
+        def several(block, inner):
+            for sub in range(unroll):
+                inner = step(block * unroll + sub, inner)
+            return inner
+
+        return lax.fori_loop(0, LEV // unroll, several, carry)
+
+    level_copy.wait()
+    area_level_copy.wait()
     lev = levels[...]
     wet0 = lev > 0
 
+    def widen(x):
+        return jnp.concatenate([x, jnp.zeros((rows, LANES - cols), x.dtype)], axis=1)
+
+    area_lev = widen(area_levels_in[...])
+    vel_copy.wait()
+    vel[...] = vel_in[...].astype(jnp.float32)
+
     def add_level(k, carry):
         su, sv, depth, area_depth = carry
-        t = coef[0, k]
+        t = at_level(0, k)
         wet = jnp.where(lev > k, t, 0.0)
-        su = su + wet * vel[0, k].astype(jnp.float32)
-        sv = sv + wet * vel[1, k].astype(jnp.float32)
-        area_depth = area_depth + jnp.where(area_levels[...] > k, t, 0.0)
+        uu, vv = pair(vel, k)
+        su = su + wet * uu
+        sv = sv + wet * vv
+        t = jnp.broadcast_to(coef[0, pl.ds(k, 1), :], (rows, LANES))
+        area_depth = area_depth + jnp.where(area_lev > k, t, 0.0)
         return su, sv, depth + wet, area_depth
 
     zero = jnp.zeros((brows, LANES), jnp.float32)
-    sum_u, sum_v, depth, area_depth = lax.fori_loop(
-        0, LEV, add_level, (zero, zero, zero, jnp.zeros((rows, LANES), jnp.float32))
+    sum_u, sum_v, depth, area_depth = sweep(
+        add_level, (zero, zero, zero, jnp.zeros((rows, LANES), jnp.float32)), 6
     )
+    forcing_copy.wait()
     wind_x = jnp.where(wet0, forcing[0], 0.0)
     wind_y = jnp.where(wet0, forcing[1], 0.0)
     payload = jnp.concatenate([sum_u, sum_v, wind_x, wind_y], axis=0)
 
+    def by_lanes(x):
+        return jnp.concatenate([x[r : r + 1] for r in range(x.shape[0])], axis=1)
+
     def slots(start, size):
-        idx = slot_idx[:, start : start + size]
+        idx = by_lanes(send_in[start // LANES : (start + size) // LANES, :])
         return idx >> 7, one_hot(idx & (LANES - 1))
 
+    def own_slots():
+        halves = LANES // cols
+        got = [own_in[pl.ds(h, rows // halves, stride=halves), :] for h in range(halves)]
+        idx = by_lanes(jnp.concatenate(got, axis=1))
+        return idx >> 7, one_hot(idx & (LANES - 1))
+
+    def cell_parts(idx):
+        return lax.div(idx + cols, cols) - 1, one_hot(lax.rem(idx + cols, cols))
+
     def cells(start, size):
-        idx = cell_idx[:, start : start + size]
-        return lax.div(idx + cols, cols) - 1, one_hot(lax.rem(idx + cols, cols))
+        return cell_parts(by_lanes(receive_in[start // LANES : (start + size) // LANES, :]))
 
     chunk = min(1024, remote)
     per_chunk = chunk // LANES
@@ -205,6 +305,7 @@
             [a2a_in[stage, first // LANES + block] for block in range(per_chunk)], axis=1
         )
 
+    send_copy.wait()
     for first in chunks:
         row_idx, hot = slots(first, chunk)
         stage_out(0, first, pack(payload, 4, row_idx, hot))
@@ -287,10 +388,19 @@
                 )
                 win[stage * 4 + f, (dx + 2) * rows : (dx + 3) * rows, :] = block
 
-    state_tiles = [area[0], area[1], area[2], area_depth]
+    height_copy.wait()
+    transport_copy.wait()
+    state_tiles = [
+        widen(height_in[...]),
+        widen(transport_in[0]),
+        widen(transport_in[1]),
+        area_depth,
+    ]
     start_halo(0, state_tiles)
 
-    inv_top = coef[3, 0]
+    trc_copy.wait()
+    trc[...] = trc_in[...].astype(jnp.float32)
+    inv_top = 1.0 / at_level(0, 0)
     heat = jnp.where(wet0, time_step * inv_top * forcing[2], 0.0)
     salt = jnp.where(wet0, time_step * inv_top * forcing[3], 0.0)
     push_x = time_step * inv_top * wind_x
@@ -303,28 +413,28 @@
     def first_forward(k, carry):
         ratio, u, v, a, b = carry
         wet = lev > k
-        low = jnp.where(wet, -coef[1, k], 0.0)
-        upp = jnp.where(lev > k + 1, -coef[2, k], 0.0)
+        low = jnp.where(wet, -at_level(1, k), 0.0)
+        upp = jnp.where(lev > k + 1, -at_level(2, k), 0.0)
         inv = 1.0 / (1.0 - low - upp - low * ratio)
         ratio = upp * inv
         low_inv = low * inv
         ratio_s[k] = ratio
         low_s[k] = low_inv
         inv_s[k] = inv
-        uu = vel[0, k].astype(jnp.float32)
-        vv = vel[1, k].astype(jnp.float32)
+        uu, vv = pair(vel, k)
+        aa, bb = pair(trc, k)
         wet_inv = jnp.where(wet, inv, 0.0)
         u = (uu + tilt * vv + top_term(k, push_x)) * wet_inv - low_inv * u
         v = (vv - tilt * uu + top_term(k, push_y)) * wet_inv - low_inv * v
-        a = (trc[0, k].astype(jnp.float32) + top_term(k, heat)) * wet_inv - low_inv * a
-        b = (trc[1, k].astype(jnp.float32) + top_term(k, salt)) * wet_inv - low_inv * b
+        a = (aa + top_term(k, heat)) * wet_inv - low_inv * a
+        b = (bb + top_term(k, salt)) * wet_inv - low_inv * b
         val[0, k] = u
         val[1, k] = v
         val[2, k] = a
         val[3, k] = b
         return ratio, u, v, a, b
 
-    lax.fori_loop(0, LEV, first_forward, (zero, zero, zero, zero, zero))
+    sweep(first_forward, (zero, zero, zero, zero, zero), 4)
 
     def gather_area():
         total = None
@@ -334,9 +444,11 @@
             total = term if total is None else total + term
         return total
 
-    own_row, own_hot = slots(remote, local)
+    own_copy.wait()
+    receive_copy.wait()
+    own_row, own_hot = own_slots()
     own_vals = pack(payload, 4, own_row, own_hot)
-    cell_row, cell_hot = cells(remote, local)
+    cell_row, cell_hot = cell_parts(lax.broadcasted_iota(jnp.int32, (1, local), 1))
     own_area = unpack(own_vals, rows, cell_row, cell_hot)
     finish_exchange(0)
     tile = own_area + gather_area()
@@ -347,7 +459,7 @@
         k = LEV - 1 - step
         u, v, a, b, du, dv = carry
         ratio = ratio_s[k]
-        t = coef[0, k]
+        t = at_level(0, k)
         u = val[0, k] - ratio * u
         v = val[1, k] - ratio * v
         a = val[2, k] - ratio * a
@@ -358,44 +470,8 @@
         val[3, k] = b
         return u, v, a, b, du + t * u, dv + t * v
 
-    mixed = lax.fori_loop(0, LEV, first_backward, (zero,) * 6)
+    mixed = sweep(first_backward, (zero,) * 6, 6)
     first_du, first_dv = mixed[4], mixed[5]
-
-    def second_forward(k, carry):
-        u, v, a, b = carry
-        low_inv = low_s[k]
-        wet_inv = jnp.where(lev > k, inv_s[k], 0.0)
-        uu = val[0, k]
-        vv = val[1, k]
-        u = (uu + tilt * vv + top_term(k, push_x)) * wet_inv - low_inv * u
-        v = (vv - tilt * uu + top_term(k, push_y)) * wet_inv - low_inv * v
-        a = (val[2, k] + top_term(k, heat)) * wet_inv - low_inv * a
-        b = (val[3, k] + top_term(k, salt)) * wet_inv - low_inv * b
-        val[0, k] = u
-        val[1, k] = v
-        val[2, k] = a
-        val[3, k] = b
-        return u, v, a, b
-
-    lax.fori_loop(0, LEV, second_forward, (zero,) * 4)
-
-    def second_backward(step, carry):
-        k = LEV - 1 - step
-        u, v, a, b, du, dv = carry
-        ratio = ratio_s[k]
-        t = coef[0, k]
-        u = val[0, k] - ratio * u
-        v = val[1, k] - ratio * v
-        a = val[2, k] - ratio * a
-        b = val[3, k] - ratio * b
-        val[0, k] = u
-        val[1, k] = v
-        out_trc[0, k] = a.astype(jnp.bfloat16)
-        out_trc[1, k] = b.astype(jnp.bfloat16)
-        return u, v, a, b, du + t * u, dv + t * v
-
-    mixed = lax.fori_loop(0, LEV, second_backward, (zero,) * 6)
-    second_du, second_dv = mixed[4], mixed[5]
 
     finish_halo(0, state_tiles)
     finish_halo(1, sum_tiles)
@@ -446,8 +522,45 @@
         row_idx, hot = cells(first, chunk)
         stage_out(1, first, pack(flow, 4, row_idx, hot))
     start_exchange(1)
-    for f in range(3):
-        out_area[f] = centre(state[f])
+    def second_forward(k, carry):
+        u, v, a, b = carry
+        low_inv = low_s[k]
+        wet_inv = jnp.where(lev > k, inv_s[k], 0.0)
+        uu = val[0, k]
+        vv = val[1, k]
+        u = (uu + tilt * vv + top_term(k, push_x)) * wet_inv - low_inv * u
+        v = (vv - tilt * uu + top_term(k, push_y)) * wet_inv - low_inv * v
+        a = (val[2, k] + top_term(k, heat)) * wet_inv - low_inv * a
+        b = (val[3, k] + top_term(k, salt)) * wet_inv - low_inv * b
+        val[0, k] = u
+        val[1, k] = v
+        val[2, k] = a
+        val[3, k] = b
+        return u, v, a, b
+
+    sweep(second_forward, (zero,) * 4, 6)
+
+    def second_backward(step, carry):
+        k = LEV - 1 - step
+        u, v, a, b, du, dv = carry
+        ratio = ratio_s[k]
+        t = at_level(0, k)
+        u = val[0, k] - ratio * u
+        v = val[1, k] - ratio * v
+        a = val[2, k] - ratio * a
+        b = val[3, k] - ratio * b
+        val[0, k] = u
+        val[1, k] = v
+        put_pair(trc, k, a, b)
+        return u, v, a, b, du + t * u, dv + t * v
+
+    mixed = sweep(second_backward, (zero,) * 6, 6)
+    second_du, second_dv = mixed[4], mixed[5]
+
+    out_trc[...] = trc[...].astype(jnp.bfloat16)
+    out_height[...] = centre(state[0])[:, :cols]
+    out_transport[0] = centre(state[1])[:, :cols]
+    out_transport[1] = centre(state[2])[:, :cols]
     slot_flow = unpack(pack(flow, 4, cell_row, cell_hot), brows, own_row, own_hot)
     finish_exchange(1)
     for first in chunks:
@@ -464,11 +577,38 @@
 
     def finish(k, carry):
         wet = lev > k
-        out_vel[0, k] = (val[0, k] + jnp.where(wet, last_u, 0.0)).astype(jnp.bfloat16)
-        out_vel[1, k] = (val[1, k] + jnp.where(wet, last_v, 0.0)).astype(jnp.bfloat16)
+        put_pair(
+            vel,
+            k,
+            val[0, k] + jnp.where(wet, last_u, 0.0),
+            val[1, k] + jnp.where(wet, last_v, 0.0),
+        )
         return carry
 
-    lax.fori_loop(0, LEV, finish, 0)
+    sweep(finish, 0, 6)
+    out_vel[...] = vel[...].astype(jnp.bfloat16)
+
+
+def deliver(*refs):
+    count = (len(refs) - 1) // 2
+    sems = refs[-1]
+    copies = [
+        pltpu.make_async_copy(refs[i], refs[count + i], sems.at[i]) for i in range(count)
+    ]
+    for copy in copies:
+        copy.start()
+    for copy in copies:
+        copy.wait()
+
+
+def flat(x, brows):
+    x = x.reshape(2, LEV, brows, LANES)
+    return jnp.transpose(x, (1, 2, 0, 3)).reshape(LEV * brows * 2, LANES)
+
+
+def unflat(x, brows):
+    x = x.reshape(LEV, brows, 2, LANES)
+    return jnp.transpose(x, (2, 0, 1, 3)).reshape(2, LEV, 1, brows * LANES)
 
 
 def body(
@@ -490,43 +630,47 @@
     slots = levels.shape[1]
     brows = slots // LANES
     cap = send_list.shape[3]
-    vel = velocity.reshape(2, LEV, brows, LANES)
-    trc = tracers.reshape(2, LEV, brows, LANES)
     forcing = surface_forcing.reshape(4, brows, LANES)
-    gap = (0.5 * 2.0 * mixing) / (thickness[:-1] + thickness[1:])
-    none = jnp.zeros((1,), jnp.float32)
-    coef = jnp.stack(
-        [
-            thickness,
-            jnp.concatenate([none, gap]) / thickness,
-            jnp.concatenate([gap, none]) / thickness,
-            1.0 / thickness,
-        ]
+    pad = ((0, 0), (0, 0), (0, LANES - cap))
+    sends, receives = send_list[0], receive_cell[0]
+    if cap < LANES:
+        sends = jnp.pad(sends, pad, constant_values=-1)
+        receives = jnp.pad(receives, pad, constant_values=-1)
+    operands = (
+        thickness.reshape(1, LEV),
+        flat(velocity, brows),
+        flat(tracers, brows),
+        forcing,
+        levels.reshape(brows, LANES),
+        surface_levels,
+        height,
+        transport,
+        sends[0],
+        receives[0],
+        own_slot,
     )
-    pad = ((0, 0), (0, 0), (0, LANES - cap))
-    sends = jnp.pad(send_list[0], pad, constant_values=-1).reshape(1, -1)
-    receives = jnp.pad(receive_cell[0], pad, constant_values=-1).reshape(1, -1)
-    slot_idx = jnp.concatenate([sends, own_slot.reshape(1, -1)], axis=1)
-    cell_idx = jnp.concatenate(
-        [receives, lax.broadcasted_iota(jnp.int32, (1, rows * cols), 1)], axis=1
-    )
-    area = jnp.concatenate([height[None], transport], axis=0)
-    area = jnp.pad(area, ((0, 0), (0, 0), (0, LANES - cols)))
-    area_levels = jnp.pad(surface_levels, ((0, 0), (0, LANES - cols)))
     vmem = pl.BlockSpec(memory_space=pltpu.VMEM)
-    smem = pl.BlockSpec(memory_space=pltpu.SMEM)
+    hbm = pl.BlockSpec(memory_space=pltpu.HBM)
     f32 = jnp.float32
     column = pltpu.VMEM((LEV, brows, LANES), f32)
-    new_vel, new_trc, new_area = pl.pallas_call(
+    whole = (LEV * brows * 2, LANES)
+    results = (
+        jax.ShapeDtypeStruct(whole, jnp.bfloat16),
+        jax.ShapeDtypeStruct(whole, jnp.bfloat16),
+        jax.ShapeDtypeStruct((rows, cols), f32),
+        jax.ShapeDtypeStruct((2, rows, cols), f32),
+    )
+    got = pl.pallas_call(
         functools.partial(kernel, n_tx, n_ty),
-        out_shape=(
-            jax.ShapeDtypeStruct((2, LEV, brows, LANES), jnp.bfloat16),
-            jax.ShapeDtypeStruct((2, LEV, brows, LANES), jnp.bfloat16),
-            jax.ShapeDtypeStruct((3, rows, LANES), f32),
-        ),
-        in_specs=[smem] + [vmem] * 8,
-        out_specs=(vmem, vmem, vmem),
-        scratch_shapes=[
+        out_shape=results,
+        in_specs=[hbm] * len(operands),
+        out_specs=(vmem,) * 4,
+        scratch_shapes=[pltpu.VMEM(x.shape, x.dtype) for x in operands]
+        + [
+            pltpu.SemaphoreType.DMA((len(operands),)),
+            pltpu.VMEM((3, 64, LANES), f32),
+            pltpu.VMEM(whole, f32),
+            pltpu.VMEM(whole, f32),
             column,
             column,
             column,
@@ -548,10 +692,16 @@
             collective_id=0, has_side_effects=True, vmem_limit_bytes=48 * 1024 * 1024
         ),
         name="ocean",
-    )(coef, vel, trc, forcing, levels.reshape(brows, LANES), area_levels, area, slot_idx, cell_idx)
-    new_velocity = new_vel.reshape(2, LEV, 1, slots)
-    new_tracers = new_trc.reshape(2, LEV, 1, slots)
-    return (new_velocity, new_tracers, new_area[0, :, :cols], new_area[1:, :, :cols])
+    )(*[pltpu.with_memory_space_constraint(x, pltpu.HBM) for x in operands])
+    new_vel, new_trc, new_height, new_transport = pl.pallas_call(
+        deliver,
+        out_shape=results,
+        in_specs=[vmem] * 4,
+        out_specs=(hbm,) * 4,
+        scratch_shapes=[pltpu.SemaphoreType.DMA((4,))],
+        name="deliver",
+    )(*[pltpu.with_memory_space_constraint(x, pltpu.VMEM) for x in got])
+    return (unflat(new_vel, brows), unflat(new_trc, brows), new_height, new_transport)
 
 
 def solution(mesh):

time: 34.2 us -> 24.7 us (0.72)
  local copies, waits for them, and re-layouts: 9.01 us -> 0 us
    unnamed x22 -> x0, local copies, waits for them, and re-layouts: 6.15 us -> none
    reshape x7 -> x0, local copies, waits for them, and re-layouts: 1.64 us -> none  [the longest x2 1.12 us: body(): vel = velocity.reshape(2, LEV, brows, LANES)]
    slice x1 -> x0, local copies, waits for them, and re-layouts: 0.61 us -> none  [body(): new_area[1:, :, :cols]]
    squeeze x1 -> x0, local copies, waits for them, and re-layouts: 0.6 us -> none  [body(): new_area[0, :, :cols]]
    pallas_call x1 -> x2, Pallas kernels: 23.8 us -> 23.9 us  [the longest x1 23.1 us: body(): pl.pallas_call(functools.partial(kernel, n_tx, n_ty), out_shape=results,...]
where the time goes in v1:
time: 24.7 us; the launch traced here: 24.5 us
  Pallas kernels  23.9 us (97%)
  between operations  0.64 us (3%)
    pallas_call x1, Pallas kernels, body(): pl.pallas_call(functools.partial(kernel, n_tx, n_ty), out_shape=results,...  23.1 us
    pallas_call x1, Pallas kernels, body(): pl.pallas_call(deliver, out_shape=results, in_specs=[vmem] * 4, out_specs...  0.82 us

profile of v1, /device:TPU:0, one launch (start us, length us, event | category | flops | bytes accessed | tf_op | source)
XLA Modules:
  0.0 24.5 jit_solution(8827249265783820923)
XLA Ops:
  0.6 23.1 %ocean.1 = (bf16[960,128]{1,0:T(8,128)(2,1)S(1)}, bf16[960,128]{1,0:T(8,128)(2,1)S(1)}, f32[16,64]{1,0:T(8,128)S(1)}, f32[2,16,64]{2,1,0:T(8,128)S(1)}) custom-call(f32[1,60]{1,0:T(1,128)} %bitcast.31, bf16[960,128]{1,0:T(8,128)(2,1)} %bitcast.25, bf16[960,128]{1,0:T(8,128)(2,1)} %bitcast.26, f32[4,8,128]{2,1,0:T(8,128)} %bitcast.27, s32[8,128]{1,0:T(8,128)} %bitcast.28, ...), custom_call_target="tpu_custom_call" | custom-call | tf_op jit(solution)/shard_map/ocean/pallas_call | solution.py:663
  23.7 0.8 %deliver.1 = (bf16[960,128]{1,0:T(8,128)(2,1)}, bf16[960,128]{1,0:T(8,128)(2,1)}, f32[16,64]{1,0:T(8,128)}, f32[2,16,64]{2,1,0:T(8,128)}) custom-call(bf16[960,128]{1,0:T(8,128)(2,1)S(1)} %get-tuple-element.12.refs_0_, bf16[960,128]{1,0:T(8,128)(2,1)S(1)} %get-tuple-element.13.refs_1_, f32[16,64]{1,0:T(8,128)S(1)} %get-tuple-element.14.refs_2_, ...), custom_call_target="tpu_custom_call" | custom-call | tf_op jit(solution)/shard_map/deliver/pallas_call | solution.py:696

commit v2 on v1

--- a/solution.py
+++ b/solution.py
@@ -306,8 +306,8 @@
         )
 
     send_copy.wait()
-    for first in chunks:
-        row_idx, hot = slots(first, chunk)
+    slot_maps = [slots(first, chunk) for first in chunks]
+    for first, (row_idx, hot) in zip(chunks, slot_maps):
         stage_out(0, first, pack(payload, 4, row_idx, hot))
 
     greeted = jnp.int32(n_tx - 1)
@@ -438,8 +438,7 @@
 
     def gather_area():
         total = None
-        for first in chunks:
-            row_idx, hot = cells(first, chunk)
+        for first, (row_idx, hot) in zip(chunks, cell_maps):
             term = unpack(stage_in(0, first), rows, row_idx, hot)
             total = term if total is None else total + term
         return total
@@ -447,6 +446,7 @@
     own_copy.wait()
     receive_copy.wait()
     own_row, own_hot = own_slots()
+    cell_maps = [cells(first, chunk) for first in chunks]
     own_vals = pack(payload, 4, own_row, own_hot)
     cell_row, cell_hot = cell_parts(lax.broadcasted_iota(jnp.int32, (1, local), 1))
     own_area = unpack(own_vals, rows, cell_row, cell_hot)
@@ -479,47 +479,65 @@
     depth_w = win[3]
     rate = transport_rate / LEV
     face_e = jnp.minimum(depth_w, pltpu.roll(depth_w, wrows - 1, 0))
-    face_n = jnp.minimum(depth_w, pltpu.roll(depth_w, LANES - 1, 1))
-    rate_e = rate * face_e
-    rate_n = rate * face_n
-    su, sv, wx, wy = win[4], win[5], win[6], win[7]
-    state = (win[0], win[1], win[2])
+    face_n = jnp.minimum(depth_w, roll_lanes(depth_w, -1))
+    filled = depth_w / jnp.maximum(depth_w, depth_floor)
+    statics = (rate * face_e, rate * face_n, filled, win[4], win[5], win[6], win[7])
+    state = (win[0], roll_lanes(win[0], -1), win[1], win[2])
+    shrink = 8
     means = []
-    filled = depth_w / jnp.maximum(depth_w, depth_floor)
+
+    def inner(x):
+        return x[shrink : x.shape[0] - shrink]
+
     for ocean_step in range(STEPS):
+        rate_e, rate_n, filled, su, sv, wx, wy = statics
         force_e = coriolis * sv + wx
         force_n = wy - coriolis * su
-        push_e = rate * force_e
-        push_n = rate * force_n
-
-        def substep(counter, carry):
-            h, e, n, te, tn = carry
-            spread = e - pltpu.roll(e, 1, 0) + n - pltpu.roll(n, 1, 1)
-            h = h - height_rate * spread
-            slope_e = pltpu.roll(h, wrows - 1, 0) - h
-            slope_n = pltpu.roll(h, LANES - 1, 1) - h
-            e = jnp.where(rate_e > 0, e + (push_e - rate_e * slope_e), 0.0)
-            n = jnp.where(rate_n > 0, n + (push_n - rate_n * slope_n), 0.0)
-            return h, e, n, te + e, tn + n
-
-        nothing = jnp.zeros((wrows, LANES), jnp.float32)
-        h, e, n, te, tn = lax.fori_loop(0, NSUB, substep, state + (nothing, nothing))
-        state = (h, e, n)
-        mean_e = te / NSUB
-        mean_n = tn / NSUB
+        push = (rate * force_e, rate * force_n)
+        flow_sum = (jnp.zeros_like(force_e), jnp.zeros_like(force_e))
+        for part in range(NSUB // shrink):
+            rate_e, rate_n = statics[:2]
+            push_e, push_n = push
+            size = rate_e.shape[0]
+
+            def substep(carry, rate_e=rate_e, rate_n=rate_n, push_e=push_e, push_n=push_n, size=size):
+                h, h_next, e, n, te, tn = carry
+                e_next = roll_lanes(e, -1)
+                h = h - height_rate * (e - pltpu.roll(e, 1, 0) + n - roll_lanes(n, 1))
+                h_next = h_next - height_rate * (
+                    e_next - pltpu.roll(e_next, 1, 0) + roll_lanes(n, -1) - n
+                )
+                slope_e = pltpu.roll(h, size - 1, 0) - h
+                slope_n = h_next - h
+                e = jnp.where(rate_e > 0, e + (push_e - rate_e * slope_e), 0.0)
+                n = jnp.where(rate_n > 0, n + (push_n - rate_n * slope_n), 0.0)
+                return h, h_next, e, n, te + e, tn + n
+
+            def two(counter, carry, substep=substep):
+                return substep(substep(carry))
+
+            carry = lax.fori_loop(0, shrink // 2, two, state + flow_sum)
+            carry = tuple(inner(x) for x in carry)
+            statics = tuple(inner(x) for x in statics)
+            push = tuple(inner(x) for x in push)
+            state, flow_sum = carry[:4], carry[4:]
+        mean_e = flow_sum[0] / NSUB
+        mean_n = flow_sum[1] / NSUB
         means += [mean_e, mean_n]
         if ocean_step + 1 < STEPS:
-            du = su + time_step * force_e
-            dv = sv + time_step * force_n
+            rate_e, rate_n, filled, su, sv, wx, wy = statics
+            du = su + time_step * (coriolis * sv + wx)
+            dv = sv + time_step * (wy - coriolis * su)
             su = du + (mean_e - du) * filled
             sv = dv + (mean_n - dv) * filled
+            statics = (rate_e, rate_n, filled, su, sv, wx, wy)
 
     def centre(x):
-        return roll_lanes(x[2 * rows : 3 * rows], -HALO)
+        first = (x.shape[0] - rows) // 2
+        return roll_lanes(x[first : first + rows], -HALO)
 
     flow = jnp.concatenate([centre(x) for x in means], axis=0)
-    for first in chunks:
-        row_idx, hot = cells(first, chunk)
+    for first, (row_idx, hot) in zip(chunks, cell_maps):
         stage_out(1, first, pack(flow, 4, row_idx, hot))
     start_exchange(1)
     def second_forward(k, carry):
@@ -559,12 +577,11 @@
 
     out_trc[...] = trc[...].astype(jnp.bfloat16)
     out_height[...] = centre(state[0])[:, :cols]
-    out_transport[0] = centre(state[1])[:, :cols]
-    out_transport[1] = centre(state[2])[:, :cols]
+    out_transport[0] = centre(state[2])[:, :cols]
+    out_transport[1] = centre(state[3])[:, :cols]
     slot_flow = unpack(pack(flow, 4, cell_row, cell_hot), brows, own_row, own_hot)
     finish_exchange(1)
-    for first in chunks:
-        row_idx, hot = slots(first, chunk)
+    for first, (row_idx, hot) in zip(chunks, slot_maps):
         slot_flow = slot_flow + unpack(stage_in(1, first), brows, row_idx, hot)
 
     floor = jnp.maximum(depth, depth_floor)

time: 24.7 us -> 22.7 us (0.919)
  Pallas kernels: 23.9 us -> 21.9 us
    pallas_call x1, Pallas kernels: 23.1 us -> 21.1 us  [body(): pl.pallas_call(functools.partial(kernel, n_tx, n_ty), out_shape=results,...]
where the time goes in v2:
time: 22.7 us; the launch traced here: 22.6 us
  Pallas kernels  21.9 us (96%)
  between operations  0.64 us (3%)
    pallas_call x1, Pallas kernels, body(): pl.pallas_call(functools.partial(kernel, n_tx, n_ty), out_shape=results,...  21.1 us
    pallas_call x1, Pallas kernels, body(): pl.pallas_call(deliver, out_shape=results, in_specs=[vmem] * 4, out_specs...  0.82 us

profile of v2, /device:TPU:0, one launch (start us, length us, event | category | flops | bytes accessed | tf_op | source)
XLA Modules:
  0.0 22.6 jit_solution(34801832728329849)
XLA Ops:
  0.6 21.1 %ocean.1 = (bf16[960,128]{1,0:T(8,128)(2,1)S(1)}, bf16[960,128]{1,0:T(8,128)(2,1)S(1)}, f32[16,64]{1,0:T(8,128)S(1)}, f32[2,16,64]{2,1,0:T(8,128)S(1)}) custom-call(f32[1,60]{1,0:T(1,128)} %bitcast.31, bf16[960,128]{1,0:T(8,128)(2,1)} %bitcast.25, bf16[960,128]{1,0:T(8,128)(2,1)} %bitcast.26, f32[4,8,128]{2,1,0:T(8,128)} %bitcast.27, s32[8,128]{1,0:T(8,128)} %bitcast.28, ...), custom_call_target="tpu_custom_call" | custom-call | tf_op jit(solution)/shard_map/ocean/pallas_call | solution.py:680
  21.7 0.8 %deliver.1 = (bf16[960,128]{1,0:T(8,128)(2,1)}, bf16[960,128]{1,0:T(8,128)(2,1)}, f32[16,64]{1,0:T(8,128)}, f32[2,16,64]{2,1,0:T(8,128)}) custom-call(bf16[960,128]{1,0:T(8,128)(2,1)S(1)} %get-tuple-element.12.refs_0_, bf16[960,128]{1,0:T(8,128)(2,1)S(1)} %get-tuple-element.13.refs_1_, f32[16,64]{1,0:T(8,128)S(1)} %get-tuple-element.14.refs_2_, ...), custom_call_target="tpu_custom_call" | custom-call | tf_op jit(solution)/shard_map/deliver/pallas_call | solution.py:713

commit v3 on v2

--- a/solution.py
+++ b/solution.py
@@ -410,31 +410,17 @@
     def top_term(k, x):
         return jnp.where(k == 0, x, 0.0)
 
-    def first_forward(k, carry):
-        ratio, u, v, a, b = carry
-        wet = lev > k
-        low = jnp.where(wet, -at_level(1, k), 0.0)
+    def coefficients(k, ratio):
+        low = jnp.where(lev > k, -at_level(1, k), 0.0)
         upp = jnp.where(lev > k + 1, -at_level(2, k), 0.0)
         inv = 1.0 / (1.0 - low - upp - low * ratio)
         ratio = upp * inv
-        low_inv = low * inv
         ratio_s[k] = ratio
-        low_s[k] = low_inv
+        low_s[k] = low * inv
         inv_s[k] = inv
-        uu, vv = pair(vel, k)
-        aa, bb = pair(trc, k)
-        wet_inv = jnp.where(wet, inv, 0.0)
-        u = (uu + tilt * vv + top_term(k, push_x)) * wet_inv - low_inv * u
-        v = (vv - tilt * uu + top_term(k, push_y)) * wet_inv - low_inv * v
-        a = (aa + top_term(k, heat)) * wet_inv - low_inv * a
-        b = (bb + top_term(k, salt)) * wet_inv - low_inv * b
-        val[0, k] = u
-        val[1, k] = v
-        val[2, k] = a
-        val[3, k] = b
-        return ratio, u, v, a, b
-
-    sweep(first_forward, (zero, zero, zero, zero, zero), 4)
+        return ratio
+
+    sweep(coefficients, zero, 6)
 
     def gather_area():
         total = None
@@ -454,6 +440,26 @@
     tile = own_area + gather_area()
     sum_tiles = [tile[f * rows : (f + 1) * rows] for f in range(4)]
     start_halo(1, sum_tiles)
+
+    finish_halo(0, state_tiles)
+
+    def first_forward(k, carry):
+        u, v, a, b = carry
+        low_inv = low_s[k]
+        wet_inv = jnp.where(lev > k, inv_s[k], 0.0)
+        uu, vv = pair(vel, k)
+        aa, bb = pair(trc, k)
+        u = (uu + tilt * vv + top_term(k, push_x)) * wet_inv - low_inv * u
+        v = (vv - tilt * uu + top_term(k, push_y)) * wet_inv - low_inv * v
+        a = (aa + top_term(k, heat)) * wet_inv - low_inv * a
+        b = (bb + top_term(k, salt)) * wet_inv - low_inv * b
+        val[0, k] = u
+        val[1, k] = v
+        val[2, k] = a
+        val[3, k] = b
+        return u, v, a, b
+
+    sweep(first_forward, (zero,) * 4, 6)
 
     def first_backward(step, carry):
         k = LEV - 1 - step
@@ -473,7 +479,6 @@
     mixed = sweep(first_backward, (zero,) * 6, 6)
     first_du, first_dv = mixed[4], mixed[5]
 
-    finish_halo(0, state_tiles)
     finish_halo(1, sum_tiles)
     wrows = 5 * rows
     depth_w = win[3]
@@ -513,10 +518,10 @@
                 n = jnp.where(rate_n > 0, n + (push_n - rate_n * slope_n), 0.0)
                 return h, h_next, e, n, te + e, tn + n
 
-            def two(counter, carry, substep=substep):
-                return substep(substep(carry))
-
-            carry = lax.fori_loop(0, shrink // 2, two, state + flow_sum)
+            def four(counter, carry, substep=substep):
+                return substep(substep(substep(substep(carry))))
+
+            carry = lax.fori_loop(0, shrink // 4, four, state + flow_sum)
             carry = tuple(inner(x) for x in carry)
             statics = tuple(inner(x) for x in statics)
             push = tuple(inner(x) for x in push)

time: 22.7 us -> 22.6 us (level)
  no operation moved by 1% of the time
where the time goes in v3:
time: 22.6 us; the launch traced here: 22.4 us
  Pallas kernels  21.8 us (96%)
  between operations  0.64 us (3%)
    pallas_call x1, Pallas kernels, body(): pl.pallas_call(functools.partial(kernel, n_tx, n_ty), out_shape=results,...  21 us
    pallas_call x1, Pallas kernels, body(): pl.pallas_call(deliver, out_shape=results, in_specs=[vmem] * 4, out_specs...  0.82 us

profile of v3, /device:TPU:0, one launch (start us, length us, event | category | flops | bytes accessed | tf_op | source)
XLA Modules:
  0.0 22.4 jit_solution(2673777114350233903)
XLA Ops:
  0.6 21.0 %ocean.1 = (bf16[960,128]{1,0:T(8,128)(2,1)S(1)}, bf16[960,128]{1,0:T(8,128)(2,1)S(1)}, f32[16,64]{1,0:T(8,128)S(1)}, f32[2,16,64]{2,1,0:T(8,128)S(1)}) custom-call(f32[1,60]{1,0:T(1,128)} %bitcast.31, bf16[960,128]{1,0:T(8,128)(2,1)} %bitcast.25, bf16[960,128]{1,0:T(8,128)(2,1)} %bitcast.26, f32[4,8,128]{2,1,0:T(8,128)} %bitcast.27, s32[8,128]{1,0:T(8,128)} %bitcast.28, ...), custom_call_target="tpu_custom_call" | custom-call | tf_op jit(solution)/shard_map/ocean/pallas_call | solution.py:685
  21.6 0.8 %deliver.1 = (bf16[960,128]{1,0:T(8,128)(2,1)}, bf16[960,128]{1,0:T(8,128)(2,1)}, f32[16,64]{1,0:T(8,128)}, f32[2,16,64]{2,1,0:T(8,128)}) custom-call(bf16[960,128]{1,0:T(8,128)(2,1)S(1)} %get-tuple-element.12.refs_0_, bf16[960,128]{1,0:T(8,128)(2,1)S(1)} %get-tuple-element.13.refs_1_, f32[16,64]{1,0:T(8,128)S(1)} %get-tuple-element.14.refs_2_, ...), custom_call_target="tpu_custom_call" | custom-call | tf_op jit(solution)/shard_map/deliver/pallas_call | solution.py:718

commit v4 on v3

--- a/solution.py
+++ b/solution.py
@@ -185,13 +185,7 @@
         return jnp.broadcast_to(column, (size, LANES))
 
     thick = along_rows(row)
-    gap = jnp.where(
-        lane_at[:1] < LEV - 1, mixing / (row + pltpu.roll(row, LANES - 1, 1)), 0.0
-    )
     coef[0] = thick
-    coef[1] = along_rows(pltpu.roll(gap, 1, 1)) / thick
-    coef[2] = along_rows(gap) / thick
-
     def at_level(which, k):
         return jnp.broadcast_to(coef[which, pl.ds(k, 1), :], (brows, LANES))
 
@@ -216,59 +210,52 @@
         return lax.fori_loop(0, LEV // unroll, several, carry)
 
     level_copy.wait()
-    area_level_copy.wait()
     lev = levels[...]
     wet0 = lev > 0
 
-    def widen(x):
-        return jnp.concatenate([x, jnp.zeros((rows, LANES - cols), x.dtype)], axis=1)
-
-    area_lev = widen(area_levels_in[...])
+    def by_lanes(x):
+        return jnp.concatenate([x[r : r + 1] for r in range(x.shape[0])], axis=1)
+
+    def slots(start, size):
+        idx = by_lanes(send_in[start // LANES : (start + size) // LANES, :])
+        return idx >> 7, one_hot(idx & (LANES - 1))
+
+    def own_slots():
+        halves = LANES // cols
+        got = [own_in[pl.ds(h, rows // halves, stride=halves), :] for h in range(halves)]
+        idx = by_lanes(jnp.concatenate(got, axis=1))
+        return idx >> 7, one_hot(idx & (LANES - 1))
+
+    def cell_parts(idx):
+        return lax.div(idx + cols, cols) - 1, one_hot(lax.rem(idx + cols, cols))
+
+    def cells(start, size):
+        return cell_parts(by_lanes(receive_in[start // LANES : (start + size) // LANES, :]))
+
+    chunk = min(1024, remote)
+    per_chunk = chunk // LANES
+    chunks = range(0, remote, chunk)
+
+    send_copy.wait()
+    slot_maps = [slots(first, chunk) for first in chunks]
     vel_copy.wait()
     vel[...] = vel_in[...].astype(jnp.float32)
 
     def add_level(k, carry):
-        su, sv, depth, area_depth = carry
+        su, sv, depth = carry
         t = at_level(0, k)
         wet = jnp.where(lev > k, t, 0.0)
         uu, vv = pair(vel, k)
         su = su + wet * uu
         sv = sv + wet * vv
-        t = jnp.broadcast_to(coef[0, pl.ds(k, 1), :], (rows, LANES))
-        area_depth = area_depth + jnp.where(area_lev > k, t, 0.0)
-        return su, sv, depth + wet, area_depth
+        return su, sv, depth + wet
 
     zero = jnp.zeros((brows, LANES), jnp.float32)
-    sum_u, sum_v, depth, area_depth = sweep(
-        add_level, (zero, zero, zero, jnp.zeros((rows, LANES), jnp.float32)), 6
-    )
+    sum_u, sum_v, depth = sweep(add_level, (zero, zero, zero), 10)
     forcing_copy.wait()
     wind_x = jnp.where(wet0, forcing[0], 0.0)
     wind_y = jnp.where(wet0, forcing[1], 0.0)
     payload = jnp.concatenate([sum_u, sum_v, wind_x, wind_y], axis=0)
-
-    def by_lanes(x):
-        return jnp.concatenate([x[r : r + 1] for r in range(x.shape[0])], axis=1)
-
-    def slots(start, size):
-        idx = by_lanes(send_in[start // LANES : (start + size) // LANES, :])
-        return idx >> 7, one_hot(idx & (LANES - 1))
-
-    def own_slots():
-        halves = LANES // cols
-        got = [own_in[pl.ds(h, rows // halves, stride=halves), :] for h in range(halves)]
-        idx = by_lanes(jnp.concatenate(got, axis=1))
-        return idx >> 7, one_hot(idx & (LANES - 1))
-
-    def cell_parts(idx):
-        return lax.div(idx + cols, cols) - 1, one_hot(lax.rem(idx + cols, cols))
-
-    def cells(start, size):
-        return cell_parts(by_lanes(receive_in[start // LANES : (start + size) // LANES, :]))
-
-    chunk = min(1024, remote)
-    per_chunk = chunk // LANES
-    chunks = range(0, remote, chunk)
 
     def exchange_copy(stage, peer, mine):
         return pltpu.make_async_remote_copy(
@@ -305,8 +292,6 @@
             [a2a_in[stage, first // LANES + block] for block in range(per_chunk)], axis=1
         )
 
-    send_copy.wait()
-    slot_maps = [slots(first, chunk) for first in chunks]
     for first, (row_idx, hot) in zip(chunks, slot_maps):
         stage_out(0, first, pack(payload, 4, row_idx, hot))
 
@@ -388,6 +373,16 @@
                 )
                 win[stage * 4 + f, (dx + 2) * rows : (dx + 3) * rows, :] = block
 
+    area_level_copy.wait()
+    def widen(x):
+        return jnp.concatenate([x, jnp.zeros((rows, LANES - cols), x.dtype)], axis=1)
+
+    area_lev = widen(area_levels_in[...])
+    def add_area_level(k, area_depth):
+        t = jnp.broadcast_to(coef[0, pl.ds(k, 1), :], (rows, LANES))
+        return area_depth + jnp.where(area_lev > k, t, 0.0)
+
+    area_depth = sweep(add_area_level, jnp.zeros((rows, LANES), jnp.float32), 10)
     height_copy.wait()
     transport_copy.wait()
     state_tiles = [
@@ -397,6 +392,12 @@
         area_depth,
     ]
     start_halo(0, state_tiles)
+
+    gap = jnp.where(
+        lane_at[:1] < LEV - 1, mixing / (row + pltpu.roll(row, LANES - 1, 1)), 0.0
+    )
+    coef[1] = along_rows(pltpu.roll(gap, 1, 1)) / thick
+    coef[2] = along_rows(gap) / thick
 
     trc_copy.wait()
     trc[...] = trc_in[...].astype(jnp.float32)

time: 22.6 us -> 22.6 us (level)
  no operation moved by 1% of the time
where the time goes in v4:
time: 22.6 us; the launch traced here: 22.4 us
  Pallas kernels  21.8 us (96%)
  between operations  0.64 us (3%)
    pallas_call x1, Pallas kernels, body(): pl.pallas_call(functools.partial(kernel, n_tx, n_ty), out_shape=results,...  21 us
    pallas_call x1, Pallas kernels, body(): pl.pallas_call(deliver, out_shape=results, in_specs=[vmem] * 4, out_specs...  0.82 us

profile of v4, /device:TPU:0, one launch (start us, length us, event | category | flops | bytes accessed | tf_op | source)
XLA Modules:
  0.0 22.4 jit_solution(17490615071693329556)
XLA Ops:
  0.6 21.0 %ocean.1 = (bf16[960,128]{1,0:T(8,128)(2,1)S(1)}, bf16[960,128]{1,0:T(8,128)(2,1)S(1)}, f32[16,64]{1,0:T(8,128)S(1)}, f32[2,16,64]{2,1,0:T(8,128)S(1)}) custom-call(f32[1,60]{1,0:T(1,128)} %bitcast.31, bf16[960,128]{1,0:T(8,128)(2,1)} %bitcast.25, bf16[960,128]{1,0:T(8,128)(2,1)} %bitcast.26, f32[4,8,128]{2,1,0:T(8,128)} %bitcast.27, s32[8,128]{1,0:T(8,128)} %bitcast.28, ...), custom_call_target="tpu_custom_call" | custom-call | tf_op jit(solution)/shard_map/ocean/pallas_call | solution.py:686
  21.6 0.8 %deliver.1 = (bf16[960,128]{1,0:T(8,128)(2,1)}, bf16[960,128]{1,0:T(8,128)(2,1)}, f32[16,64]{1,0:T(8,128)}, f32[2,16,64]{2,1,0:T(8,128)}) custom-call(bf16[960,128]{1,0:T(8,128)(2,1)S(1)} %get-tuple-element.12.refs_0_, bf16[960,128]{1,0:T(8,128)(2,1)S(1)} %get-tuple-element.13.refs_1_, f32[16,64]{1,0:T(8,128)S(1)} %get-tuple-element.14.refs_2_, ...), custom_call_target="tpu_custom_call" | custom-call | tf_op jit(solution)/shard_map/deliver/pallas_call | solution.py:719
